TPU v7x, 512 devices: a whole 4x8x8 slice. The times are simulated.
512 devices in a mesh: dp: 128 (over z, y, core), tensor: 4 (over x).
Axes of the slice: x: 4, y: 8, z: 8, core: 2. Of those that a mesh axis runs over, the one named last changes fastest.
Arguments:
- hidden: bfloat16 [65536, 1024], P('dp', 'tensor'), may hold values from -24 to 24
- gain: float32 [1024], replicated, may hold values from 0.5 to 1.5
- head_weight: bfloat16 [1024, 25600], P(None, ('tensor', 'dp')), may hold values from -6 to 6
- targets: int32 [65536], P('dp'), may hold values from 0 to 25599
- row_count: int32 [128], P('dp'), may hold values from 64 to 512, as said below
- dest: int32 [65536], P('dp'), may hold values from 0 to 65535, as said below
Outputs:
- logprob: float32 [65536], P('dp')
- entropy: float32 [65536], P('dp')
Inputs may be any that keep to these rules, and one draw needn't show every extreme that they name: Each device's live slots are its first row_count ones; at least one device is full. dest is a permutation. Slot results of device s go to device dest // 512; every device sends exactly 4 results to every device, those from device s fill positions s * 4 to (s + 1) * 4 - 1 of the receiver's block, in the order of their position in the sender's slots sorted by destination.
All inputs are finite; a program needn't handle non-finite values.
Results may differ from a plain program's by a relative error of at most 0.0062.
Values may be sent and summed in bfloat16 or wider, within the bound.
A program may use at most 128 MiB of HBM per device.

v0:
```python
import jax
import jax.numpy as jnp
from jax import lax
from jax.sharding import Mesh, PartitionSpec as P


def stats_of(logits_t, wanted):
    top = jnp.max(logits_t, axis=0)
    weights = jnp.exp(logits_t - top[None, :])
    mass = jnp.sum(weights, axis=0)
    moment = jnp.sum(weights * logits_t, axis=0)
    ids = lax.broadcasted_iota(jnp.int32, logits_t.shape, 0)
    picked = jnp.sum(jnp.where(ids == wanted[None, :], logits_t, 0.0), axis=0)
    return jnp.stack([top, mass, moment, picked])


def merge(parts):
    top = jnp.max(parts[:, 0], axis=0)
    factor = jnp.exp(parts[:, 0] - top[None])
    mass = jnp.sum(parts[:, 1] * factor, axis=0)
    moment = jnp.sum(parts[:, 2] * factor, axis=0)
    return (top, mass, moment, jnp.sum(parts[:, 3], axis=0))


def body(hidden, gain, head_weight, targets, row_count, dest):
    rows = hidden.shape[0]
    cols = head_weight.shape[1]
    padded = -(-cols // 8) * 8
    groups = lax.axis_size("zy") * 2
    tensors = lax.axis_size("tensor")
    core = lax.axis_index("core")
    mine = lax.axis_index("tensor")
    swap = [(0, 1), (1, 0)]
    spread = jnp.pad(head_weight.T, ((0, padded - cols), (0, 0)))
    piece = lax.all_gather(spread, "zy", axis=0, tiled=True)
    shards = [hidden]
    for step in range(1, tensors):
        shards.append(
            lax.ppermute(hidden, "tensor", [((i + step) % tensors, i) for i in range(tensors)])
        )
    own = jnp.stack(shards)
    other = lax.ppermute(own, "core", swap)
    both = jnp.concatenate([own, other], axis=1).astype(jnp.float32)
    power = jnp.sum(both * both, axis=(0, 2)) / (tensors * hidden.shape[1])
    scale = lax.rsqrt(power + 1e-06)
    gains = jnp.roll(gain.reshape(tensors, -1), -mine, axis=0)
    turned = (both * scale[None, :, None] * gains[:, None, :]).astype(jnp.bfloat16)
    ordered = jnp.roll(turned, mine, axis=0)
    normed = jnp.moveaxis(ordered, 0, 1).reshape(2 * rows, -1)
    wanted = jnp.concatenate([targets, lax.ppermute(targets, "core", swap)])
    local = wanted - mine * (cols * groups)
    device = local // cols
    ok = (local >= 0) & (device < groups) & (device % 2 == core)
    slot = jnp.where(ok, device // 2 * padded + local % cols, -1)
    logits = lax.dot_general(
        piece, normed, (((1,), (1,)), ((), ())), preferred_element_type=jnp.float32
    )
    ids = lax.broadcasted_iota(jnp.int32, logits.shape, 0)
    logits = jnp.where(ids % padded < cols, logits, -1e30)
    stats = stats_of(logits, slot)
    theirs = lax.ppermute(stats[:, rows:], "core", swap)
    pair = jnp.stack(merge(jnp.stack([stats[:, :rows], theirs])))
    top, mass, moment, picked = merge(lax.all_gather(pair, "tensor", axis=0))
    live = jnp.arange(rows, dtype=jnp.int32) < row_count[0]
    lse = top + jnp.log(mass)
    value_lp = jnp.where(live, picked - lse, 0.0)
    value_ent = jnp.where(live, lse - moment / mass, 0.0)
    share = rows // groups
    rank = dest // rows * share + dest % share
    hit = lax.broadcasted_iota(jnp.int32, (rows, rows), 0) == rank[None, :]
    sent = [
        jnp.sum(jnp.where(hit, v[None, :], 0.0), axis=1).reshape(groups, share)
        for v in (value_lp, value_ent)
    ]
    got = lax.all_to_all(jnp.concatenate(sent, axis=1), ("zy", "core"), 0, 0, tiled=True)
    return (got[:, :share].reshape(rows), got[:, share:].reshape(rows))


def solution(mesh):
    dp, tensor = mesh.devices.shape
    fine = Mesh(mesh.devices.reshape(dp // 2, 2, tensor), ("zy", "core", "tensor"))
    group = ("zy", "core")
    in_specs = (
        P(group, "tensor"),
        P(),
        P(None, ("tensor", "zy", "core")),
        P(group),
        P(group),
        P(group),
    )
    return jax.shard_map(
        body, mesh=fine, in_specs=in_specs, out_specs=(P(group), P(group)), check_vma=False
    )
```

profile of v0, /device:TPU:1, one launch (start us, length us, event | category | flops | bytes accessed | tf_op | source)
XLA Modules:
  0.0 172.6 jit_solution(16111850264375092905)
XLA Ops:
  7.2 1.6 pad.4
  8.8 1.1 copy.31
  9.9 5.2 %collective-permute-start = (bf16[512,256]{0,1:T(8,128)(2,1)S(1)}, bf16[512,256]{0,1:T(8,128)(2,1)S(1)}, u32[]{:S(2)}, u32[]{:S(2)}) collective-permute-start(bf16[512,256]{0,1:T(8,128)(2,1)S(1)} %copy.31), channel_id=1, source_target_pairs={{1,0},{2,1},{3,2},{0,3},{5,4},{6,5},{7,6},{4,7},{9,8},{10,9},{11,1... | collective-permute-start | bytes 786440 | tf_op jit(solution)/shard_map/ppermute | solution.py:39
  15.1 2.4 %collective-permute-start.1 = (bf16[512,256]{0,1:T(8,128)(2,1)S(1)}, bf16[512,256]{0,1:T(8,128)(2,1)S(1)}, u32[]{:S(2)}, u32[]{:S(2)}) collective-permute-start(bf16[512,256]{0,1:T(8,128)(2,1)S(1)} %copy.31), channel_id=1, source_target_pairs={{2,0},{3,1},{0,2},{1,3},{6,4},{7,5},{4,6},{5,7},{10,8},{11,9},{8,1... | collective-permute-start | bytes 786440 | tf_op jit(solution)/shard_map/ppermute | solution.py:39
  17.5 2.5 %collective-permute-start.2 = (bf16[512,256]{0,1:T(8,128)(2,1)S(1)}, bf16[512,256]{0,1:T(8,128)(2,1)S(1)}, u32[]{:S(2)}, u32[]{:S(2)}) collective-permute-start(bf16[512,256]{0,1:T(8,128)(2,1)S(1)} %copy.31), channel_id=1, source_target_pairs={{3,0},{0,1},{1,2},{2,3},{7,4},{4,5},{5,6},{6,7},{11,8},{8,9},{9,10... | collective-permute-start | bytes 786440 | tf_op jit(solution)/shard_map/ppermute | solution.py:39
  20.1 3.7 %collective-permute-done.1 = bf16[512,256]{0,1:T(8,128)(2,1)S(1)} collective-permute-done((bf16[512,256]{0,1:T(8,128)(2,1)S(1)}, bf16[512,256]{0,1:T(8,128)(2,1)S(1)}, u32[]{:S(2)}, u32[]{:S(2)}) %collective-permute-start.1) | collective-permute-done | bytes 262176 | tf_op jit(solution)/shard_map/ppermute | solution.py:39
  23.8 4.7 %collective-permute-done.2 = bf16[512,256]{0,1:T(8,128)(2,1)S(1)} collective-permute-done((bf16[512,256]{0,1:T(8,128)(2,1)S(1)}, bf16[512,256]{0,1:T(8,128)(2,1)S(1)}, u32[]{:S(2)}, u32[]{:S(2)}) %collective-permute-start.2) | collective-permute-done | bytes 262176 | tf_op jit(solution)/shard_map/ppermute | solution.py:39
  28.6 6.2 %collective-permute-start.3 = (bf16[4,512,256]{1,2,0:T(8,128)(2,1)S(1)}, bf16[4,512,256]{1,2,0:T(8,128)(2,1)S(1)}, u32[]{:S(2)}, u32[]{:S(2)}) collective-permute-start(bf16[4,512,256]{1,2,0:T(8,128)(2,1)S(1)} %pad_maximum_fusion.1), channel_id=1, source_target_pairs={{0,4},{4,0},{1,5},{5,1},{2,6},{6,2},{3,7},{7,3},{8,12},{12,8},{9,1... | collective-permute-start | bytes 3145736 | tf_op jit(solution)/shard_map/ppermute | solution.py:42
  34.9 1.9 %collective-permute-start.4 = (s32[512]{0:T(512)}, s32[512]{0:T(512)S(1)}, u32[]{:S(2)}, u32[]{:S(2)}) collective-permute-start(s32[512]{0:T(512)} %param.9), channel_id=1, source_target_pairs={{0,4},{4,0},{1,5},{5,1},{2,6},{6,2},{3,7},{7,3},{8,12},{12,8},{9,1... | collective-permute-start | bytes 6152 | tf_op jit(solution)/shard_map/ppermute | solution.py:50
  36.8 0.7 reshape.120
  37.6 0.5 collective-permute-done.4
  38.2 0.7 fusion.21
  38.9 0.5 fusion.2
  39.4 0.6 fusion.4
  40.0 0.8 fusion.5
  40.8 69.9 %all-gather.4.cloned.1.call-done = bf16[3584,1024]{1,0:T(8,128)(2,1)} async-done(((bf16[56,1024]{1,0:T(8,128)(2,1)}), bf16[3584,1024]{1,0:T(8,128)(2,1)}) %all-gather.4.cloned.1.call-update) | async-done | bytes 7340048 | tf_op jit(solution)/shard_map/all_gather | solution.py:35
  110.7 10.5 %fusion.40 = (f32[1024]{0:T(1024)S(1)}, f32[3584,1024]{1,0:T(8,128)S(1)}) fusion(bf16[3584,1024]{1,0:T(8,128)(2,1)} %all-gather.4.cloned.1.call-done, bf16[1024,1024]{0,1:T(8,128)(2,1)S(1)} %bitcast.76, s32[3584]{0:T(1024)S(1)} %get-tuple-element.29, s32[3584]{0:T(1024)S(1)} %get-tuple-element.30, pred[3584]{0:T(1024)(128)(4,1)S(1)} %fusion.9), kind=kOutput, calls=%fused_computation.97 | convolution fusion | flops 7530871808 | bytes 24153600 | tf_op jit(solution)/shard_map/dot_general | solution.py:55
  121.1 4.8 %fusion = (f32[1024]{0:T(1024)S(1)}, f32[1024]{0:T(1024)S(1)}, f32[1024]{0:T(1024)S(1)}) fusion(f32[3584,1024]{1,0:T(8,128)S(1)} %get-tuple-element.28, f32[1024]{0:T(1024)S(1)} %get-tuple-element.27, s32[1024]{0:T(1024)S(1)} %fusion.21), kind=kLoop, calls=%fused_computation.4 | loop fusion | flops 25687040 | bytes 14700544 | tf_op jit(solution)/shard_map/reduce_sum | solution.py:10
  126.0 3.0 %collective-permute-start.5 = (f32[4,512]{1,0:T(4,128)S(1)}, f32[4,512]{1,0:T(4,128)S(1)}, u32[]{:S(2)}, u32[]{:S(2)}) collective-permute-start(f32[4,512]{1,0:T(4,128)S(1)} %get-tuple-element.24), channel_id=1, source_target_pairs={{0,4},{4,0},{1,5},{5,1},{2,6},{6,2},{3,7},{7,3},{8,12},{12,8},{9,1... | collective-permute-start | bytes 24584 | tf_op jit(solution)/shard_map/ppermute | solution.py:61
  130.0 9.3 %all-gather.1 = f32[4,4,512]{2,1,0:T(4,128)S(1)} all-gather(f32[1,4,512]{2,1,0:T(4,128)S(1)} %maximum_bitcast_fusion), channel_id=2, replica_groups=mesh['zy'=64,'core'=2,'tensor'=4] {'tensor'}, dimensions={0}, use_global_device_ids=true | all-gather | bytes 40960 | tf_op jit(solution)/shard_map/all_gather | solution.py:63
  139.4 0.4 select_reduce_fusion.2
  140.1 24.2 %all_to_all.12 = f32[128,1,8]{2,1,0:T(1,128)S(1)} all-to-all(f32[128,1,8]{2,1,0:T(1,128)S(1)} %bitcast.78), channel_id=1, replica_groups=mesh['zy'=64,'core'=2,'tensor'=4] {'zy','core'}, dimensions={0} | all-to-all | bytes 8192 | tf_op jit(solution)/shard_map/all_to_all | solution.py:75
  164.4 0.7 reshape.124
  165.1 0.7 reshape.125
  (27 shorter events, 0.9 us)
Async XLA Ops:
  7.2 103.5 %all-gather.4.cloned.1.call-start = ((), (), s32[]{:S(2)}) async-start(), calls=%async_computation.1 | async-start | bytes 7454720 | tf_op jit(solution)/shard_map/all_gather | solution.py:35
  9.9 10.2 %collective-permute-start = (bf16[512,256]{0,1:T(8,128)(2,1)S(1)}, bf16[512,256]{0,1:T(8,128)(2,1)S(1)}, u32[]{:S(2)}, u32[]{:S(2)}) collective-permute-start(bf16[512,256]{0,1:T(8,128)(2,1)S(1)} %copy.31), channel_id=1, source_target_pairs={{1,0},{2,1},{3,2},{0,3},{5,4},{6,5},{7,6},{4,7},{9,8},{10,9},{11,1... | collective-permute-start | bytes 786440 | tf_op jit(solution)/shard_map/ppermute | solution.py:39
  15.1 8.7 %collective-permute-start.1 = (bf16[512,256]{0,1:T(8,128)(2,1)S(1)}, bf16[512,256]{0,1:T(8,128)(2,1)S(1)}, u32[]{:S(2)}, u32[]{:S(2)}) collective-permute-start(bf16[512,256]{0,1:T(8,128)(2,1)S(1)} %copy.31), channel_id=1, source_target_pairs={{2,0},{3,1},{0,2},{1,3},{6,4},{7,5},{4,6},{5,7},{10,8},{11,9},{8,1... | collective-permute-start | bytes 786440 | tf_op jit(solution)/shard_map/ppermute | solution.py:39
  17.5 11.0 %collective-permute-start.2 = (bf16[512,256]{0,1:T(8,128)(2,1)S(1)}, bf16[512,256]{0,1:T(8,128)(2,1)S(1)}, u32[]{:S(2)}, u32[]{:S(2)}) collective-permute-start(bf16[512,256]{0,1:T(8,128)(2,1)S(1)} %copy.31), channel_id=1, source_target_pairs={{3,0},{0,1},{1,2},{2,3},{7,4},{4,5},{5,6},{6,7},{11,8},{8,9},{9,10... | collective-permute-start | bytes 786440 | tf_op jit(solution)/shard_map/ppermute | solution.py:39
  28.6 10.2 %collective-permute-start.3 = (bf16[4,512,256]{1,2,0:T(8,128)(2,1)S(1)}, bf16[4,512,256]{1,2,0:T(8,128)(2,1)S(1)}, u32[]{:S(2)}, u32[]{:S(2)}) collective-permute-start(bf16[4,512,256]{1,2,0:T(8,128)(2,1)S(1)} %pad_maximum_fusion.1), channel_id=1, source_target_pairs={{0,4},{4,0},{1,5},{5,1},{2,6},{6,2},{3,7},{7,3},{8,12},{12,8},{9,1... | collective-permute-start | bytes 3145736 | tf_op jit(solution)/shard_map/ppermute | solution.py:42
  34.9 3.3 %collective-permute-start.4 = (s32[512]{0:T(512)}, s32[512]{0:T(512)S(1)}, u32[]{:S(2)}, u32[]{:S(2)}) collective-permute-start(s32[512]{0:T(512)} %param.9), channel_id=1, source_target_pairs={{0,4},{4,0},{1,5},{5,1},{2,6},{6,2},{3,7},{7,3},{8,12},{12,8},{9,1... | collective-permute-start | bytes 6152 | tf_op jit(solution)/shard_map/ppermute | solution.py:50
  121.1 7.9 %copy-start = (s32[512]{0:T(512)S(1)}, s32[512]{0:T(512)}, u32[]{:S(2)}) copy-start(s32[512]{0:T(512)} %param.11) | copy-start | bytes 6148
  126.0 3.9 %collective-permute-start.5 = (f32[4,512]{1,0:T(4,128)S(1)}, f32[4,512]{1,0:T(4,128)S(1)}, u32[]{:S(2)}, u32[]{:S(2)}) collective-permute-start(f32[4,512]{1,0:T(4,128)S(1)} %get-tuple-element.24), channel_id=1, source_target_pairs={{0,4},{4,0},{1,5},{5,1},{2,6},{6,2},{3,7},{7,3},{8,12},{12,8},{9,1... | collective-permute-start | bytes 24584 | tf_op jit(solution)/shard_map/ppermute | solution.py:61
Sparse Core Ops, SparseCore 0:
  11.0 99.6 all-gather.3
where the time goes:
time: 173 us
  waiting for transfers between devices  79 us (46%)
  blocking collectives  33.6 us (19%)
  starting transfers between devices  21.4 us (12%)
  between operations  14.9 us (9%)
  matrix products  10.5 us (6%)
  other arithmetic  8.21 us (5%)
  local copies, waits for them, and re-layouts  5.03 us (3%)
    all_gather x1, waiting for transfers between devices, body(): piece = lax.all_gather(spread, 'zy', axis=0, tiled=True)  69.9 us
    all_to_all x1, blocking collectives, body(): lax.all_to_all(jnp.concatenate(sent, axis=1), ('zy', 'core'), 0, 0, tiled...  24.2 us
    dot_general x1, matrix products, body(): lax.dot_general(piece, normed, (((1,), (1,)), ((), ())), preferred_elemen...  10.5 us
    ppermute x3, starting transfers between devices, body(): lax.ppermute(hidden, 'tensor', [((i + step) % tensors, i) for i in range(...  10.1 us
    all_gather x1, blocking collectives, body(): top, mass, moment, picked = merge(lax.all_gather(pair, 'tensor', axis=0))  9.34 us
    ppermute x3, waiting for transfers between devices, body(): lax.ppermute(hidden, 'tensor', [((i + step) % tensors, i) for i in range(...  8.43 us
    ppermute x1, starting transfers between devices, body(): other = lax.ppermute(own, 'core', swap)  6.25 us
    reduce_sum x1, other arithmetic, stats_of(): mass = jnp.sum(weights, axis=0)  4.82 us
  transfers between devices with their start and end apart: 7, of which 5 were waited for; matrix products, arithmetic and copies ran while one was open for 3% of the time, Pallas kernels for 0%

commit v1 on v0

--- a/solution.py
+++ b/solution.py
@@ -2,6 +2,7 @@
 import jax.numpy as jnp
 from jax import lax
 from jax.sharding import Mesh, PartitionSpec as P
+from jax.lax import all_to_all, psum
 
 
 def stats_of(logits_t, wanted):
@@ -32,7 +33,10 @@
     mine = lax.axis_index("tensor")
     swap = [(0, 1), (1, 0)]
     spread = jnp.pad(head_weight.T, ((0, padded - cols), (0, 0)))
-    piece = lax.all_gather(spread, "zy", axis=0, tiled=True)
+    shaped = psum(1, axis_name="zy")
+    after = jnp.stack(shaped * [spread])
+    raw_out = all_to_all(after, axis_name="zy", split_axis=0, concat_axis=0)
+    piece = jnp.concatenate(raw_out, axis=0)
     shards = [hidden]
     for step in range(1, tensors):
         shards.append(

time: 173 us -> 334 us (1.93)
  waiting for transfers between devices: 79 us -> 181 us
  blocking collectives: 33.6 us -> 92 us
  between operations: 14.9 us -> 1.59 us
  starting transfers between devices: 21.4 us -> 34.6 us
    all_to_all x0 -> x1, waiting for transfers between devices: none -> 168 us  [body(): raw_out = all_to_all(after, axis_name='zy', split_axis=0, concat_axis=0)]
    all_gather x1 -> x0, waiting for transfers between devices: 69.9 us -> none  [body(): piece = lax.all_gather(spread, 'zy', axis=0, tiled=True)]
    all_to_all x1, blocking collectives: 24.2 us -> 82.7 us  [body(): lax.all_to_all(jnp.concatenate(sent, axis=1), ('zy', 'core'), 0, 0, tiled...]
    all_to_all x0 -> x1, starting transfers between devices: none -> 17.5 us  [body(): raw_out = all_to_all(after, axis_name='zy', split_axis=0, concat_axis=0)]
    another operation x0 -> x1, local copies, waits for them, and re-layouts: none -> 3.96 us  [body(): after = jnp.stack(shaped * [spread])]
    ppermute x3, waiting for transfers between devices: 8.43 us -> 12.4 us  [body(): lax.ppermute(hidden, 'tensor', [((i + step) % tensors, i) for i in range(...]
    ppermute x1, starting transfers between devices: 6.25 us -> 2.31 us  [body(): other = lax.ppermute(own, 'core', swap)]
  transfers between devices with their start and end apart: 7 -> 7, of which waited for: 5 -> 6; matrix products, arithmetic and copies ran while one was open for 3% -> 1% of each run, Pallas kernels for 0% -> 0%
where the time goes in v1:
time: 334 us
  waiting for transfers between devices  181 us (54%)
  blocking collectives  92 us (28%)
  starting transfers between devices  34.6 us (10%)
  matrix products  10.5 us (3%)
  other arithmetic  7.53 us (2%)
  local copies, waits for them, and re-layouts  6.72 us (2%)
    all_to_all x1, waiting for transfers between devices, body(): raw_out = all_to_all(after, axis_name='zy', split_axis=0, concat_axis=0)  168 us
    all_to_all x1, blocking collectives, body(): lax.all_to_all(jnp.concatenate(sent, axis=1), ('zy', 'core'), 0, 0, tiled...  82.7 us
    all_to_all x1, starting transfers between devices, body(): raw_out = all_to_all(after, axis_name='zy', split_axis=0, concat_axis=0)  17.5 us
    ppermute x3, waiting for transfers between devices, body(): lax.ppermute(hidden, 'tensor', [((i + step) % tensors, i) for i in range(...  12.4 us
    dot_general x1, matrix products, body(): lax.dot_general(piece, normed, (((1,), (1,)), ((), ())), preferred_elemen...  10.5 us
    all_gather x1, blocking collectives, body(): top, mass, moment, picked = merge(lax.all_gather(pair, 'tensor', axis=0))  9.39 us
    ppermute x3, starting transfers between devices, body(): lax.ppermute(hidden, 'tensor', [((i + step) % tensors, i) for i in range(...  9.33 us
  transfers between devices with their start and end apart: 7, of which 6 were waited for; matrix products, arithmetic and copies ran while one was open for 1% of the time, Pallas kernels for 0%

profile of v1, /device:TPU:1, one launch (start us, length us, event | category | flops | bytes accessed | tf_op | source)
XLA Modules:
  0.0 334.0 jit_solution(12942541843424387394)
XLA Ops:
  0.6 0.9 pad.4
  1.5 4.0 %stack.38 = bf16[64,56,1024]{2,1,0:T(8,128)(2,1)} broadcast(bf16[56,1024]{1,0:T(8,128)(2,1)S(1)} %pad.4), dimensions={1,2} | broadcast | bytes 7454720 | tf_op jit(solution)/shard_map/stack | solution.py:37
  5.5 17.5 %all-to-all-start = ((bf16[64,56,1024]{2,1,0:T(8,128)(2,1)}), bf16[64,56,1024]{2,1,0:T(8,128)(2,1)}, u32[]{:S(2)}, u32[]{:S(2)}) async-start(bf16[64,56,1024]{2,1,0:T(8,128)(2,1)} %stack.38), calls=%async_computation | async-start | bytes 14680064 | tf_op jit(solution)/shard_map/all_to_all | solution.py:38
  23.2 4.4 %collective-permute-start = (bf16[512,256]{0,1:T(8,128)(2,1)S(1)}, bf16[512,256]{0,1:T(8,128)(2,1)S(1)}, u32[]{:S(2)}, u32[]{:S(2)}) collective-permute-start(bf16[512,256]{0,1:T(8,128)(2,1)S(1)} %copy.31), channel_id=1, source_target_pairs={{1,0},{2,1},{3,2},{0,3},{5,4},{6,5},{7,6},{4,7},{9,8},{10,9},{11,1... | collective-permute-start | bytes 786440 | tf_op jit(solution)/shard_map/ppermute | solution.py:43
  27.6 2.4 collective-permute-start.1
  30.0 2.5 collective-permute-start.2
  32.5 0.5 collective-permute-done
  33.0 4.7 %collective-permute-done.1 = bf16[512,256]{0,1:T(8,128)(2,1)S(1)} collective-permute-done((bf16[512,256]{0,1:T(8,128)(2,1)S(1)}, bf16[512,256]{0,1:T(8,128)(2,1)S(1)}, u32[]{:S(2)}, u32[]{:S(2)}) %collective-permute-start.1) | collective-permute-done | bytes 262176 | tf_op jit(solution)/shard_map/ppermute | solution.py:43
  37.7 7.2 %collective-permute-done.2 = bf16[512,256]{0,1:T(8,128)(2,1)S(1)} collective-permute-done((bf16[512,256]{0,1:T(8,128)(2,1)S(1)}, bf16[512,256]{0,1:T(8,128)(2,1)S(1)}, u32[]{:S(2)}, u32[]{:S(2)}) %collective-permute-start.2) | collective-permute-done | bytes 262176 | tf_op jit(solution)/shard_map/ppermute | solution.py:43
  45.0 2.3 collective-permute-start.3
  47.4 2.0 collective-permute-start.4
  49.5 0.9 collective-permute-done.4
  50.5 0.5 fusion.2
  51.0 0.6 fusion.4
  51.6 0.8 fusion.5
  52.4 167.6 %all-to-all-done = bf16[64,56,1024]{2,1,0:T(8,128)(2,1)} async-done(((bf16[64,56,1024]{2,1,0:T(8,128)(2,1)}), bf16[64,56,1024]{2,1,0:T(8,128)(2,1)}, u32[]{:S(2)}, u32[]{:S(2)}) %all-to-all-start) | async-done | bytes 7340064 | tf_op jit(solution)/shard_map/all_to_all | solution.py:38
  219.9 10.5 %fusion.40 = (f32[1024]{0:T(1024)S(1)}, f32[3584,1024]{1,0:T(8,128)S(1)}) fusion(bf16[3584,1024]{1,0:T(8,128)(2,1)} %bitcast.2, bf16[1024,1024]{0,1:T(8,128)(2,1)S(1)} %bitcast.77, s32[3584]{0:T(1024)S(1)} %get-tuple-element.29, s32[3584]{0:T(1024)S(1)} %get-tuple-element.30, pred[3584]{0:T(1024)(128)(4,1)S(1)} %fusion.9), kind=kOutput, calls=%fused_computation.97 | convolution fusion | flops 7530871808 | bytes 24153600 | tf_op jit(solution)/shard_map/dot_general | solution.py:59
  230.4 4.8 %fusion = (f32[1024]{0:T(1024)S(1)}, f32[1024]{0:T(1024)S(1)}, f32[1024]{0:T(1024)S(1)}) fusion(f32[3584,1024]{1,0:T(8,128)S(1)} %get-tuple-element.28, f32[1024]{0:T(1024)S(1)} %get-tuple-element.27, s32[1024]{0:T(1024)S(1)} %fusion.21), kind=kLoop, calls=%fused_computation.4 | loop fusion | flops 25687040 | bytes 14700544 | tf_op jit(solution)/shard_map/reduce_sum | solution.py:11
  235.3 3.5 %collective-permute-start.5 = (f32[4,512]{1,0:T(4,128)S(1)}, f32[4,512]{1,0:T(4,128)S(1)}, u32[]{:S(2)}, u32[]{:S(2)}) collective-permute-start(f32[4,512]{1,0:T(4,128)S(1)} %get-tuple-element.24), channel_id=1, source_target_pairs={{0,4},{4,0},{1,5},{5,1},{2,6},{6,2},{3,7},{7,3},{8,12},{12,8},{9,1... | collective-permute-start | bytes 24584 | tf_op jit(solution)/shard_map/ppermute | solution.py:65
  239.7 9.4 %all-gather.1 = f32[4,4,512]{2,1,0:T(4,128)S(1)} all-gather(f32[1,4,512]{2,1,0:T(4,128)S(1)} %maximum_bitcast_fusion), channel_id=2, replica_groups=mesh['zy'=64,'core'=2,'tensor'=4] {'tensor'}, dimensions={0}, use_global_device_ids=true | all-gather | bytes 40960 | tf_op jit(solution)/shard_map/all_gather | solution.py:67
  249.2 0.4 select_reduce_fusion.2
  249.9 82.7 %all_to_all.17 = f32[128,1,8]{2,1,0:T(1,128)S(1)} all-to-all(f32[128,1,8]{2,1,0:T(1,128)S(1)} %bitcast.79), channel_id=1, replica_groups=mesh['zy'=64,'core'=2,'tensor'=4] {'zy','core'}, dimensions={0} | all-to-all | bytes 8192 | tf_op jit(solution)/shard_map/all_to_all | solution.py:79
  332.6 0.7 reshape.130
  333.3 0.7 reshape.131
  (33 shorter events, 1.1 us)
Async XLA Ops:
  5.5 17.5 %copy-start = (bf16[512,256]{1,0:T(8,128)(2,1)S(1)}, bf16[512,256]{1,0:T(8,128)(2,1)}, u32[]{:S(2)}) copy-start(bf16[512,256]{1,0:T(8,128)(2,1)} %param.6) | copy-start | bytes 786436
  5.5 41.8 %copy-start.3 = (s32[512]{0:T(512)S(1)}, s32[512]{0:T(512)}, u32[]{:S(2)}) copy-start(s32[512]{0:T(512)} %param.9) | copy-start | bytes 6148
  5.5 43.9 %copy-start.1 = (f32[1024]{0:T(1024)S(1)}, f32[1024]{0:T(1024)}, u32[]{:S(2)}) copy-start(f32[1024]{0:T(1024)} %param.7) | copy-start | bytes 12292
  5.5 214.4 %all-to-all-start = ((bf16[64,56,1024]{2,1,0:T(8,128)(2,1)}), bf16[64,56,1024]{2,1,0:T(8,128)(2,1)}, u32[]{:S(2)}, u32[]{:S(2)}) async-start(bf16[64,56,1024]{2,1,0:T(8,128)(2,1)} %stack.38), calls=%async_computation | async-start | bytes 14680064 | tf_op jit(solution)/shard_map/all_to_all | solution.py:38
  23.2 9.9 %collective-permute-start = (bf16[512,256]{0,1:T(8,128)(2,1)S(1)}, bf16[512,256]{0,1:T(8,128)(2,1)S(1)}, u32[]{:S(2)}, u32[]{:S(2)}) collective-permute-start(bf16[512,256]{0,1:T(8,128)(2,1)S(1)} %copy.31), channel_id=1, source_target_pairs={{1,0},{2,1},{3,2},{0,3},{5,4},{6,5},{7,6},{4,7},{9,8},{10,9},{11,1... | collective-permute-start | bytes 786440 | tf_op jit(solution)/shard_map/ppermute | solution.py:43
  27.6 10.2 %collective-permute-start.1 = (bf16[512,256]{0,1:T(8,128)(2,1)S(1)}, bf16[512,256]{0,1:T(8,128)(2,1)S(1)}, u32[]{:S(2)}, u32[]{:S(2)}) collective-permute-start(bf16[512,256]{0,1:T(8,128)(2,1)S(1)} %copy.31), channel_id=1, source_target_pairs={{2,0},{3,1},{0,2},{1,3},{6,4},{7,5},{4,6},{5,7},{10,8},{11,9},{8,1... | collective-permute-start | bytes 786440 | tf_op jit(solution)/shard_map/ppermute | solution.py:43
  30.0 14.9 %collective-permute-start.2 = (bf16[512,256]{0,1:T(8,128)(2,1)S(1)}, bf16[512,256]{0,1:T(8,128)(2,1)S(1)}, u32[]{:S(2)}, u32[]{:S(2)}) collective-permute-start(bf16[512,256]{0,1:T(8,128)(2,1)S(1)} %copy.31), channel_id=1, source_target_pairs={{3,0},{0,1},{1,2},{2,3},{7,4},{4,5},{5,6},{6,7},{11,8},{8,9},{9,10... | collective-permute-start | bytes 786440 | tf_op jit(solution)/shard_map/ppermute | solution.py:43
  45.0 5.4 %collective-permute-start.3 = (bf16[4,512,256]{1,2,0:T(8,128)(2,1)S(1)}, bf16[4,512,256]{1,2,0:T(8,128)(2,1)S(1)}, u32[]{:S(2)}, u32[]{:S(2)}) collective-permute-start(bf16[4,512,256]{1,2,0:T(8,128)(2,1)S(1)} %pad_maximum_fusion.1), channel_id=1, source_target_pairs={{0,4},{4,0},{1,5},{5,1},{2,6},{6,2},{3,7},{7,3},{8,12},{12,8},{9,1... | collective-permute-start | bytes 3145736 | tf_op jit(solution)/shard_map/ppermute | solution.py:46
  47.4 3.1 collective-permute-start.4
  230.4 8.4 %copy-start.2 = (s32[512]{0:T(512)S(1)}, s32[512]{0:T(512)}, u32[]{:S(2)}) copy-start(s32[512]{0:T(512)} %param.11) | copy-start | bytes 6148
  235.3 4.3 %collective-permute-start.5 = (f32[4,512]{1,0:T(4,128)S(1)}, f32[4,512]{1,0:T(4,128)S(1)}, u32[]{:S(2)}, u32[]{:S(2)}) collective-permute-start(f32[4,512]{1,0:T(4,128)S(1)} %get-tuple-element.24), channel_id=1, source_target_pairs={{0,4},{4,0},{1,5},{5,1},{2,6},{6,2},{3,7},{7,3},{8,12},{12,8},{9,1... | collective-permute-start | bytes 24584 | tf_op jit(solution)/shard_map/ppermute | solution.py:65
